TPU v7x, 32 devices: a whole 2x2x4 slice. The times are simulated.
32 devices in a mesh: lon: 8 (over y, x, core), bal: 4 (over z).
Axes of the slice: x: 2, y: 2, z: 4, core: 2. Of those that a mesh axis runs over, the one named last changes fastest.
Arguments:
- conc: float32 [65536, 128], P(('lon', 'bal')), may hold values from -6 to 6
- neighbours: int32 [512, 8], P(('lon', 'bal')), may hold values from 0 to 511, as said below
- counts: int32 [512], P(('lon', 'bal')), may hold values from 1 to 8
- weights: int32 [512, 8], P(('lon', 'bal')), may hold values from 1 to 15
- zones: int32 [65536], P(('lon', 'bal')), may hold values from 0 to 31
- owners: int32 [65536, 1], P(('lon', 'bal')), may hold values from 0 to 3; in each aligned block of 2048 rows (0 to 2047, 2048 to 4095, ...) at most 1024 rows name the same one
- rate_table: float32 [32, 128], replicated, may hold values from 0.05 to 1
- reaction: bfloat16 [128, 128], replicated, may hold values from -0.5 to 0.5
Outputs:
- conc_out: bfloat16 [65536, 128], P(('lon', 'bal'))
- chem_slots: bfloat16 [131072, 128], P(('lon', 'bal'))
Inputs may be any that keep to these rules, and one draw needn't show every extreme that they name: neighbours[g, k] is a block of the same bal index as g, on the same longitude band or on the band just before or after it, with the bands wrapping around. On every trajectory owner, at most 1024 of its parcels have the same owners value; on some trajectory owners one value is taken exactly 1024 times.
All inputs are finite; a program needn't handle non-finite values.
Results may differ from a plain program's by a relative error of at most 0.0085.
Values may be sent and summed in bfloat16 or wider, within the bound.
No kernel may reach another device: no remote copies, remote signals or barrier semaphores. Data moves between devices by JAX's collectives and lax.ppermute only.
A program may use at most 64 MiB of HBM per device.

v0:
```python
import jax
import jax.numpy as jnp
from jax import lax
from jax.sharding import PartitionSpec as P

BLK = 128
KADJ = 8
ZONES = 32
SUBSTEPS = 12


def extended_2(cells, sides, width):
    for axis, dim in sides:
        count = lax.axis_size(axis)
        head = lax.slice_in_dim(cells, 0, width, axis=dim)
        tail = lax.slice_in_dim(cells, cells.shape[dim] - width, cells.shape[dim], axis=dim)
        cells = jnp.concatenate(
            [
                lax.ppermute(tail, axis, [(i, (i + 1) % count) for i in range(count)]),
                cells,
                lax.ppermute(head, axis, [((i + 1) % count, i) for i in range(count)]),
            ],
            axis=dim,
        )
    return cells


def shifted(value, axis, steps):
    count = lax.axis_size(axis)
    pairs = [(source, (source + steps) % count) for source in range(count)]
    return lax.ppermute(value, axis, pairs)


def chemistry(state, reaction):

    def advance(step_index, current):
        tendency = jnp.dot(
            current.astype(jnp.bfloat16), reaction, preferred_element_type=jnp.float32
        )
        return current + 0.25 * jnp.tanh(tendency)

    return lax.fori_loop(0, SUBSTEPS, advance, state.astype(jnp.float32)).astype(jnp.bfloat16)


def shards(conc, neighbours, counts, weights, zones, owners, rate_table, reaction):
    rows, width = conc.shape
    nblocks = rows // BLK
    lon_count = lax.axis_size("lon")
    bal_count = lax.axis_size("bal")
    device_count = lon_count * bal_count
    self_device = lax.axis_index("lon") * bal_count + lax.axis_index("bal")
    own_blocks = conc.reshape(nblocks, BLK, width)
    extended = extended_2(own_blocks, (("lon", 0),), nblocks)
    used = jnp.arange(KADJ, dtype=jnp.int32)[None, :] < counts[:, None]
    coefs = jnp.where(used, weights.astype(jnp.float32) / 128.0, 0.0)
    local_part = neighbours % nblocks
    apart = (neighbours // nblocks - self_device + device_count) % device_count
    ext_index = (
        jnp.where(apart == 0, nblocks, jnp.where(apart == bal_count, 2 * nblocks, 0)) + local_part
    )
    change = jnp.zeros((nblocks, BLK, width), jnp.float32)
    sent = jnp.zeros((3 * nblocks, BLK, width), jnp.float32)
    for column in range(KADJ):
        flux = coefs[:, column][:, None, None] * (extended[ext_index[:, column]] - own_blocks)
        change = change + flux
        sent = sent.at[ext_index[:, column]].add(flux)
    from_right = shifted(sent[:nblocks].astype(jnp.bfloat16), "lon", -1).astype(jnp.float32)
    from_left = shifted(sent[2 * nblocks :].astype(jnp.bfloat16), "lon", 1).astype(jnp.float32)
    change = change - sent[nblocks : 2 * nblocks] - from_right - from_left
    mixed = (own_blocks + change).reshape(rows, width)
    zone_table = (zones[:, None] == jnp.arange(ZONES, dtype=jnp.int32)[None, :]).astype(jnp.float32)
    rates = jnp.dot(zone_table, rate_table, precision=lax.Precision.HIGHEST)
    moved = (mixed * jnp.exp(-rates)).astype(jnp.bfloat16)
    capacity = 2 * rows // bal_count
    owner = owners[:, 0]
    owner_table = (owner[:, None] == jnp.arange(bal_count, dtype=jnp.int32)[None, :]).astype(
        jnp.int32
    )
    rank = jnp.sum((jnp.cumsum(owner_table, axis=0) - owner_table) * owner_table, axis=1)
    slot = owner * capacity + rank
    conc_out = chemistry(moved, reaction)
    outgoing = jnp.zeros((bal_count * capacity, width), jnp.bfloat16).at[slot].set(conc_out)
    outgoing = outgoing.reshape(bal_count, capacity, width)
    chem_slots = lax.all_to_all(outgoing, "bal", split_axis=0, concat_axis=0, tiled=True).reshape(
        -1, width
    )
    return (conc_out, chem_slots)


def solution(mesh):
    in_specs = (
        P(("lon", "bal"), None),
        P(("lon", "bal"), None),
        P(("lon", "bal")),
        P(("lon", "bal"), None),
        P(("lon", "bal")),
        P(("lon", "bal"), None),
        P(),
        P(),
    )
    out_specs = (P(("lon", "bal"), None), P(("lon", "bal"), None))
    return jax.shard_map(shards, mesh=mesh, in_specs=in_specs, out_specs=out_specs, check_vma=False)
```

profile of v0, /device:TPU:0, one launch (start us, length us, event | category | flops | bytes accessed | tf_op | source)
XLA Modules:
  0.0 134.0 jit_solution(15365341471317218973)
XLA Ops:
  0.6 0.5 collective-permute-start
  1.2 2.9 %collective-permute-start.1 = (f32[16,128,128]{2,1,0:T(8,128)}, f32[16,128,128]{2,1,0:T(8,128)}, u32[]{:S(2)}, u32[]{:S(2)}) collective-permute-start(f32[16,128,128]{2,1,0:T(8,128)} %bitcast.69), channel_id=1, source_target_pairs={{4,0},{8,4},{12,8},{16,12},{20,16},{24,20},{28,24},{0,28},{5,1},{9... | collective-permute-start | bytes 3145736 | tf_op jit(solution)/shard_map/ppermute | solution.py:21
  4.1 0.7 fusion.19
  4.9 0.7 fusion.15
  5.6 1.1 reduce-window.6
  6.7 0.2 slice_reduce_fusion
  6.9 0.2 reduce-window.9
  7.1 0.7 multiply_select_fusion
  7.8 0.1 add_bitcast_fusion
  7.9 17.5 %collective-permute-done = f32[16,128,128]{2,1,0:T(8,128)S(1)} collective-permute-done((f32[16,128,128]{2,1,0:T(8,128)}, f32[16,128,128]{2,1,0:T(8,128)S(1)}, u32[]{:S(2)}, u32[]{:S(2)}) %collective-permute-start) | collective-permute-done | bytes 1048608 | tf_op jit(solution)/shard_map/ppermute | solution.py:19
  25.4 1.0 copy-done.7
  26.4 0.6 collective-permute-done.1
  27.0 2.1 %pad_maximum_fusion = f32[48,128,128]{2,1,0:T(8,128)S(1)} fusion(f32[16,128,128]{2,1,0:T(8,128)} %collective-permute-done.1, f32[16,128,128]{2,1,0:T(8,128)} %bitcast.70, f32[16,128,128]{2,1,0:T(8,128)} %copy-done.7), kind=kLoop, calls=%fused_computation.21 | loop fusion | flops 1572864 | bytes 6291456 | tf_op jit(solution)/shard_map/concatenate | solution.py:17
  29.0 1.6 %gather_fusion = f32[16,128,128]{2,1,0:T(8,128)} fusion(f32[48,128,128]{2,1,0:T(8,128)S(1)} %pad_maximum_fusion, s32[1024]{0:T(1024)S(1)} %get-tuple-element.59), kind=kCustom, calls=%fused_computation | custom fusion | bytes 2097216 | tf_op jit(solution)/shard_map/gather | solution.py:64
  30.6 1.6 %gather_fusion.1 = f32[16,128,128]{2,1,0:T(8,128)} fusion(f32[48,128,128]{2,1,0:T(8,128)S(1)} %pad_maximum_fusion, s32[1024]{0:T(1024)S(1)} %get-tuple-element.58), kind=kCustom, calls=%fused_computation.1 | custom fusion | bytes 2097216 | tf_op jit(solution)/shard_map/gather | solution.py:64
  32.3 1.6 %gather_fusion.2 = f32[16,128,128]{2,1,0:T(8,128)} fusion(f32[48,128,128]{2,1,0:T(8,128)S(1)} %pad_maximum_fusion, s32[1024]{0:T(1024)S(1)} %get-tuple-element.57), kind=kCustom, calls=%fused_computation.2 | custom fusion | bytes 2097216 | tf_op jit(solution)/shard_map/gather | solution.py:64
  33.9 1.6 %gather_fusion.3 = f32[16,128,128]{2,1,0:T(8,128)} fusion(f32[48,128,128]{2,1,0:T(8,128)S(1)} %pad_maximum_fusion, s32[1024]{0:T(1024)S(1)} %get-tuple-element.56), kind=kCustom, calls=%fused_computation.3 | custom fusion | bytes 2097216 | tf_op jit(solution)/shard_map/gather | solution.py:64
  35.5 1.6 %gather_fusion.4 = f32[16,128,128]{2,1,0:T(8,128)} fusion(f32[48,128,128]{2,1,0:T(8,128)S(1)} %pad_maximum_fusion, s32[1024]{0:T(1024)S(1)} %get-tuple-element.55), kind=kCustom, calls=%fused_computation.4 | custom fusion | bytes 2097216 | tf_op jit(solution)/shard_map/gather | solution.py:64
  37.1 1.6 %gather_fusion.5 = f32[16,128,128]{2,1,0:T(8,128)} fusion(f32[48,128,128]{2,1,0:T(8,128)S(1)} %pad_maximum_fusion, s32[1024]{0:T(1024)S(1)} %get-tuple-element.54), kind=kCustom, calls=%fused_computation.5 | custom fusion | bytes 2097216 | tf_op jit(solution)/shard_map/gather | solution.py:64
  38.7 1.6 %gather_fusion.6 = f32[16,128,128]{2,1,0:T(8,128)} fusion(f32[48,128,128]{2,1,0:T(8,128)S(1)} %pad_maximum_fusion, s32[1024]{0:T(1024)S(1)} %get-tuple-element.53), kind=kCustom, calls=%fused_computation.6 | custom fusion | bytes 2097216 | tf_op jit(solution)/shard_map/gather | solution.py:64
  40.3 1.6 %gather_fusion.7 = f32[16,128,128]{2,1,0:T(8,128)} fusion(f32[48,128,128]{2,1,0:T(8,128)S(1)} %pad_maximum_fusion, s32[1024]{0:T(1024)S(1)} %get-tuple-element.52), kind=kCustom, calls=%fused_computation.7 | custom fusion | bytes 2097216 | tf_op jit(solution)/shard_map/gather | solution.py:64
  41.9 7.7 %subtract_multiply_fusion = (f32[16,128,128]{2,1,0:T(8,128)}, f32[16,128,128]{2,1,0:T(8,128)}, f32[16,128,128]{2,1,0:T(8,128)}, f32[16,128,128]{2,1,0:T(8,128)},...) fusion(f32[16,128,128]{2,1,0:T(8,128)} %gather_fusion.7, ...), kind=kLoop, calls=%fused_computation.31 | loop fusion | flops 4194304 | bytes 17826304 | tf_op jit(solution)/shard_map/mul | solution.py:64
  49.6 0.4 broadcast_in_dim.15
  50.0 2.6 %scatter_fusion = f32[48,128,128]{2,1,0:T(8,128)S(1)} fusion(f32[48,128,128]{2,1,0:T(8,128)S(1)} %broadcast_in_dim.15, s32[16]{0:T(128)S(1)} %get-tuple-element.51, f32[16,128,128]{2,1,0:T(8,128)} %get-tuple-element.35), kind=kCustom, calls=%fused_computation.8 | custom fusion | flops 262144 | bytes 3145792 | tf_op jit(solution)/shard_map/scatter-add | solution.py:66
  52.6 2.6 %scatter_fusion.1 = f32[48,128,128]{2,1,0:T(8,128)S(1)} fusion(f32[48,128,128]{2,1,0:T(8,128)S(1)} %scatter_fusion, s32[16]{0:T(128)S(1)} %get-tuple-element.50, f32[16,128,128]{2,1,0:T(8,128)} %get-tuple-element.34), kind=kCustom, calls=%fused_computation.9 | custom fusion | flops 262144 | bytes 3145792 | tf_op jit(solution)/shard_map/scatter-add | solution.py:66
  55.2 2.6 %scatter_fusion.2 = f32[48,128,128]{2,1,0:T(8,128)S(1)} fusion(f32[48,128,128]{2,1,0:T(8,128)S(1)} %scatter_fusion.1, s32[16]{0:T(128)S(1)} %get-tuple-element.49, f32[16,128,128]{2,1,0:T(8,128)} %get-tuple-element.33), kind=kCustom, calls=%fused_computation.10 | custom fusion | flops 262144 | bytes 3145792 | tf_op jit(solution)/shard_map/scatter-add | solution.py:66
  57.8 2.6 %scatter_fusion.3 = f32[48,128,128]{2,1,0:T(8,128)S(1)} fusion(f32[48,128,128]{2,1,0:T(8,128)S(1)} %scatter_fusion.2, s32[16]{0:T(128)S(1)} %get-tuple-element.48, f32[16,128,128]{2,1,0:T(8,128)} %get-tuple-element.32), kind=kCustom, calls=%fused_computation.11 | custom fusion | flops 262144 | bytes 3145792 | tf_op jit(solution)/shard_map/scatter-add | solution.py:66
  60.5 2.6 %scatter_fusion.4 = f32[48,128,128]{2,1,0:T(8,128)S(1)} fusion(f32[48,128,128]{2,1,0:T(8,128)S(1)} %scatter_fusion.3, s32[16]{0:T(128)S(1)} %get-tuple-element.47, f32[16,128,128]{2,1,0:T(8,128)} %get-tuple-element.31), kind=kCustom, calls=%fused_computation.12 | custom fusion | flops 262144 | bytes 3145792 | tf_op jit(solution)/shard_map/scatter-add | solution.py:66
  63.1 2.6 %scatter_fusion.5 = f32[48,128,128]{2,1,0:T(8,128)S(1)} fusion(f32[48,128,128]{2,1,0:T(8,128)S(1)} %scatter_fusion.4, s32[16]{0:T(128)S(1)} %get-tuple-element.46, f32[16,128,128]{2,1,0:T(8,128)} %get-tuple-element.30), kind=kCustom, calls=%fused_computation.13 | custom fusion | flops 262144 | bytes 3145792 | tf_op jit(solution)/shard_map/scatter-add | solution.py:66
  65.7 2.6 %scatter_fusion.6 = f32[48,128,128]{2,1,0:T(8,128)S(1)} fusion(f32[48,128,128]{2,1,0:T(8,128)S(1)} %scatter_fusion.5, s32[16]{0:T(128)S(1)} %get-tuple-element.45, f32[16,128,128]{2,1,0:T(8,128)} %get-tuple-element.29), kind=kCustom, calls=%fused_computation.14 | custom fusion | flops 262144 | bytes 3145792 | tf_op jit(solution)/shard_map/scatter-add | solution.py:66
  68.3 2.6 %scatter_fusion.7 = f32[48,128,128]{2,1,0:T(8,128)S(1)} fusion(f32[48,128,128]{2,1,0:T(8,128)S(1)} %scatter_fusion.6, s32[16]{0:T(128)S(1)} %get-tuple-element.44, f32[16,128,128]{2,1,0:T(8,128)} %get-tuple-element.28), kind=kCustom, calls=%fused_computation.15 | custom fusion | flops 262144 | bytes 3145792 | tf_op jit(solution)/shard_map/scatter-add | solution.py:66
  71.0 0.3 convert.4
  71.3 0.1 fusion.29
  71.3 2.9 %collective-permute-start.2 = (bf16[16,128,128]{2,1,0:T(8,128)(2,1)S(1)}, bf16[16,128,128]{2,1,0:T(8,128)(2,1)S(1)}, u32[]{:S(2)}, u32[]{:S(2)}) collective-permute-start(bf16[16,128,128]{2,1,0:T(8,128)(2,1)S(1)} %get-tuple-element.26), channel_id=1, source_target_pairs={{0,28},{4,0},{8,4},{12,8},{16,12},{20,16},{24,20},{28,24},{1,29},{... | collective-permute-start | bytes 1572872 | tf_op jit(solution)/shard_map/ppermute | solution.py:31
  74.3 12.2 %collective-permute-done.2 = bf16[16,128,128]{2,1,0:T(8,128)(2,1)S(1)} collective-permute-done((bf16[16,128,128]{2,1,0:T(8,128)(2,1)S(1)}, bf16[16,128,128]{2,1,0:T(8,128)(2,1)S(1)}, u32[]{:S(2)}, u32[]{:S(2)}) %collective-permute-start.2) | collective-permute-done | bytes 524320 | tf_op jit(solution)/shard_map/ppermute | solution.py:31
  86.5 0.4 collective-permute-done.3
  87.0 3.1 %fusion.6 = f32[16,128,128]{2,1,0:T(8,128)S(1)} fusion(f32[16,128,128]{2,1,0:T(8,128)} %bitcast.72, f32[48,128,128]{2,1,0:T(8,128)S(1)} %scatter_fusion.7, bf16[16,128,128]{2,1,0:T(8,128)(2,1)S(1)} %collective-permute-done.3, bf16[16,128,128]{2,1,0:T(8,128)(2,1)S(1)} %collective-permute-done.2, f32[16,128,128]{2,1,0:T(8,128)S(1)} %copy-done.1, ...), kind=kLoop, calls=%fused_computation.27 | loop fusion | flops 3407872 | bytes 12582912 | tf_op jit(solution)/shard_map/add | solution.py:70
  90.1 1.1 fusion.8
  91.1 4.7 %while.10 = (s32[]{:T(128)}, f32[2048,128]{1,0:T(8,128)S(1)}, bf16[128,128]{1,0:T(8,128)(2,1)S(1)}, s32[]{:T(128)}) while((s32[]{:T(128)}, f32[2048,128]{1,0:T(8,128)S(1)}, bf16[128,128]{1,0:T(8,128)(2,1)S(1)}, s32[]{:T(128)}) %tuple.53), condition=%wide.region_9.10_spmd, body=%wide.region_8.9_spmd.sunk | while | flops 67895296 | bytes 4227125 | solution.py:42
  91.2 0.1 copy.29
  91.2 0.3 fusion.38
  91.6 0.1 copy.29
  91.6 0.3 fusion.38
  92.0 0.3 fusion.38
  92.3 0.1 copy.29
  92.4 0.3 fusion.38
  92.7 0.1 copy.29
  92.8 0.3 fusion.38
  93.2 0.3 fusion.38
  93.5 0.1 copy.29
  93.6 0.3 fusion.38
  93.9 0.1 copy.29
  93.9 0.3 fusion.38
  94.3 0.1 copy.29
  94.3 0.3 fusion.38
  94.7 0.3 fusion.38
  95.1 0.3 fusion.38
  95.4 0.1 copy.29
  95.5 0.3 fusion.38
  95.8 6.8 %scatter_custom_fusion.8 = bf16[4096,128]{1,0:T(8,128)(2,1)} fusion(s32[2048]{0:T(1024)S(1)} %bitcast.77, bf16[]{:T(256)} %constant.76.clone.1, f32[2048,128]{1,0:T(8,128)S(1)} %get-tuple-element.19), kind=kCustom, calls=%fused_computation.40 | custom fusion | flops 262144 | bytes 2097154 | tf_op jit(solution)/shard_map/scatter | solution.py:82
  102.6 5.6 %all-to-all-start = ((bf16[4,1024,128]{2,1,0:T(8,128)(2,1)}), bf16[4,1024,128]{2,1,0:T(8,128)(2,1)S(1)}, u32[]{:S(2)}, u32[]{:S(2)}) async-start(bf16[4,1024,128]{2,1,0:T(8,128)(2,1)} %bitcast.23), calls=%async_computation | async-start | bytes 2097152 | tf_op jit(solution)/shard_map/all_to_all | solution.py:84
  108.2 0.8 convert_element_type.36
  109.1 24.0 %all-to-all-done = bf16[4,1024,128]{2,1,0:T(8,128)(2,1)S(1)} async-done(((bf16[4,1024,128]{2,1,0:T(8,128)(2,1)}), bf16[4,1024,128]{2,1,0:T(8,128)(2,1)S(1)}, u32[]{:S(2)}, u32[]{:S(2)}) %all-to-all-start) | async-done | bytes 1048608 | tf_op jit(solution)/shard_map/all_to_all | solution.py:84
  133.1 1.0 copy.30
  (34 shorter events, 0.4 us)
Async XLA Ops:
  0.6 89.4 %copy-start = (f32[32,128]{1,0:T(8,128)S(1)}, f32[32,128]{1,0:T(8,128)}, u32[]{:S(2)}) copy-start(f32[32,128]{1,0:T(8,128)} %param.16) | copy-start | bytes 49156
  0.6 24.8 %collective-permute-start = (f32[16,128,128]{2,1,0:T(8,128)}, f32[16,128,128]{2,1,0:T(8,128)S(1)}, u32[]{:S(2)}, u32[]{:S(2)}) collective-permute-start(f32[16,128,128]{2,1,0:T(8,128)} %bitcast.68), channel_id=1, source_target_pairs={{0,4},{4,8},{8,12},{12,16},{16,20},{20,24},{24,28},{28,0},{1,5},{5... | collective-permute-start | bytes 3145736 | tf_op jit(solution)/shard_map/ppermute | solution.py:19
  1.2 25.8 %collective-permute-start.1 = (f32[16,128,128]{2,1,0:T(8,128)}, f32[16,128,128]{2,1,0:T(8,128)}, u32[]{:S(2)}, u32[]{:S(2)}) collective-permute-start(f32[16,128,128]{2,1,0:T(8,128)} %bitcast.69), channel_id=1, source_target_pairs={{4,0},{8,4},{12,8},{16,12},{20,16},{24,20},{28,24},{0,28},{5,1},{9... | collective-permute-start | bytes 3145736 | tf_op jit(solution)/shard_map/ppermute | solution.py:21
  25.4 1.0 copy-start.7
  70.9 3.3 %copy-start.9 = (s32[2048,1]{0,1:T(1,128)S(1)}, s32[2048,1]{0,1:T(1,128)}, u32[]{:S(2)}) copy-start(s32[2048,1]{0,1:T(1,128)} %param.15) | copy-start | bytes 24580
  70.9 16.0 %copy-start.1 = (f32[16,128,128]{2,1,0:T(8,128)S(1)}, f32[16,128,128]{2,1,0:T(8,128)}, u32[]{:S(2)}) copy-start(f32[16,128,128]{2,1,0:T(8,128)} %get-tuple-element.28) | copy-start | bytes 3145732
  70.9 16.0 %copy-start.2 = (f32[16,128,128]{2,1,0:T(8,128)S(1)}, f32[16,128,128]{2,1,0:T(8,128)}, u32[]{:S(2)}) copy-start(f32[16,128,128]{2,1,0:T(8,128)} %get-tuple-element.29) | copy-start | bytes 3145732
  71.0 16.0 %copy-start.3 = (f32[16,128,128]{2,1,0:T(8,128)S(1)}, f32[16,128,128]{2,1,0:T(8,128)}, u32[]{:S(2)}) copy-start(f32[16,128,128]{2,1,0:T(8,128)} %get-tuple-element.30) | copy-start | bytes 3145732
  71.0 16.0 %copy-start.4 = (f32[16,128,128]{2,1,0:T(8,128)S(1)}, f32[16,128,128]{2,1,0:T(8,128)}, u32[]{:S(2)}) copy-start(f32[16,128,128]{2,1,0:T(8,128)} %get-tuple-element.31) | copy-start | bytes 3145732
  71.0 16.0 %copy-start.5 = (f32[16,128,128]{2,1,0:T(8,128)S(1)}, f32[16,128,128]{2,1,0:T(8,128)}, u32[]{:S(2)}) copy-start(f32[16,128,128]{2,1,0:T(8,128)} %get-tuple-element.32) | copy-start | bytes 3145732
  71.0 16.0 %copy-start.6 = (f32[16,128,128]{2,1,0:T(8,128)S(1)}, f32[16,128,128]{2,1,0:T(8,128)}, u32[]{:S(2)}) copy-start(f32[16,128,128]{2,1,0:T(8,128)} %get-tuple-element.33) | copy-start | bytes 3145732
  71.3 15.2 %collective-permute-start.2 = (bf16[16,128,128]{2,1,0:T(8,128)(2,1)S(1)}, bf16[16,128,128]{2,1,0:T(8,128)(2,1)S(1)}, u32[]{:S(2)}, u32[]{:S(2)}) collective-permute-start(bf16[16,128,128]{2,1,0:T(8,128)(2,1)S(1)} %get-tuple-element.26), channel_id=1, source_target_pairs={{0,28},{4,0},{8,4},{12,8},{16,12},{20,16},{24,20},{28,24},{1,29},{... | collective-permute-start | bytes 1572872 | tf_op jit(solution)/shard_map/ppermute | solution.py:31
  74.2 12.7 %collective-permute-start.3 = (bf16[16,128,128]{2,1,0:T(8,128)(2,1)S(1)}, bf16[16,128,128]{2,1,0:T(8,128)(2,1)S(1)}, u32[]{:S(2)}, u32[]{:S(2)}) collective-permute-start(bf16[16,128,128]{2,1,0:T(8,128)(2,1)S(1)} %get-tuple-element.27), channel_id=1, source_target_pairs={{0,4},{4,8},{8,12},{12,16},{16,20},{20,24},{24,28},{28,0},{1,5},{5... | collective-permute-start | bytes 1572872 | tf_op jit(solution)/shard_map/ppermute | solution.py:31
  74.3 15.8 %copy-start.10 = (s32[2048]{0:T(1024)S(1)}, s32[2048]{0:T(1024)}, u32[]{:S(2)}) copy-start(s32[2048]{0:T(1024)} %param.14) | copy-start | bytes 24580
  74.3 16.8 %copy-start.8 = (bf16[128,128]{1,0:T(8,128)(2,1)S(1)}, bf16[128,128]{1,0:T(8,128)(2,1)}, u32[]{:S(2)}) copy-start(bf16[128,128]{1,0:T(8,128)(2,1)} %param.17) | copy-start | bytes 98308
  102.6 30.5 %all-to-all-start = ((bf16[4,1024,128]{2,1,0:T(8,128)(2,1)}), bf16[4,1024,128]{2,1,0:T(8,128)(2,1)S(1)}, u32[]{:S(2)}, u32[]{:S(2)}) async-start(bf16[4,1024,128]{2,1,0:T(8,128)(2,1)} %bitcast.23), calls=%async_computation | async-start | bytes 2097152 | tf_op jit(solution)/shard_map/all_to_all | solution.py:84
where the time goes:
time: 135 us; the launch traced here: 134 us
  waiting for transfers between devices  54.7 us (41%)
  other arithmetic  45.2 us (33%)
  local copies, waits for them, and re-layouts  16.3 us (12%)
  starting transfers between devices  12 us (9%)
  matrix products  4.52 us (3%)
    all_to_all x1, waiting for transfers between devices, shards(): lax.all_to_all(outgoing, 'bal', split_axis=0, concat_axis=0, tiled=True)  24 us
    scatter-add x8, other arithmetic, shards(): sent = sent.at[ext_index[:, column]].add(flux)  20.9 us
    ppermute x1, waiting for transfers between devices, extended_2(): lax.ppermute(tail, axis, [(i, (i + 1) % count) for i in range(count)])  17.5 us
    gather x8, local copies, waits for them, and re-layouts, shards(): extended[ext_index[:, column]] - own_blocks  12.9 us
    ppermute x2, waiting for transfers between devices, shifted(): return lax.ppermute(value, axis, pairs)  12.6 us
    mul x1, other arithmetic, shards(): coefs[:, column][:, None, None]  7.75 us
    scatter x1, other arithmetic, shards(): jnp.zeros((bal_count * capacity, width), jnp.bfloat16).at[slot]  6.78 us
    all_to_all x1, starting transfers between devices, shards(): lax.all_to_all(outgoing, 'bal', split_axis=0, concat_axis=0, tiled=True)  5.63 us
  transfers between devices with their start and end apart: 5, of which 5 were waited for; matrix products, arithmetic and copies ran while one was open for 3% of the time, Pallas kernels for 0%

commit v1 on v0

--- a/solution.py
+++ b/solution.py
@@ -7,6 +7,28 @@
 KADJ = 8
 ZONES = 32
 SUBSTEPS = 12
+
+
+def cut_along(value, dim, count):
+    before, after = (value.shape[:dim], value.shape[dim + 1 :])
+    return jnp.moveaxis(value.reshape(*before, count, -1, *after), dim, 0)
+
+
+def laid_out(blocks, dim):
+    shape = list(blocks.shape[1:])
+    shape[dim] *= blocks.shape[0]
+    return jnp.moveaxis(blocks, 0, dim).reshape(shape)
+
+
+def swapped_with_each(x, axis, split_dim, concat_dim):
+    peers, index = (lax.axis_size(axis), lax.axis_index(axis))
+    blocks = cut_along(x, split_dim, peers)
+    done = [blocks[index]]
+    for step in range(1, peers):
+        sent = blocks[index ^ step]
+        done.append(lax.ppermute(sent, axis, [(i, i ^ step) for i in range(peers)]))
+    blocks = jnp.stack(done)[index ^ jnp.arange(peers)]
+    return laid_out(blocks, concat_dim)
 
 
 def extended_2(cells, sides, width):
@@ -81,9 +103,7 @@
     conc_out = chemistry(moved, reaction)
     outgoing = jnp.zeros((bal_count * capacity, width), jnp.bfloat16).at[slot].set(conc_out)
     outgoing = outgoing.reshape(bal_count, capacity, width)
-    chem_slots = lax.all_to_all(outgoing, "bal", split_axis=0, concat_axis=0, tiled=True).reshape(
-        -1, width
-    )
+    chem_slots = swapped_with_each(outgoing, "bal", 0, 0).reshape(-1, width)
     return (conc_out, chem_slots)
 
 

time: 135 us -> 130 us (0.963); the launches traced: 134 us -> 127 us
  waiting for transfers between devices: 54.7 us -> 48.6 us
    all_to_all x1 -> x0, waiting for transfers between devices: 24 us -> none  [shards(): lax.all_to_all(outgoing, 'bal', split_axis=0, concat_axis=0, tiled=True)]
    ppermute x0 -> x3, waiting for transfers between devices: none -> 17.9 us  [swapped_with_each(): done.append(lax.ppermute(sent, axis, [(i, i ^ step) for i in range(peers)]))]
    all_to_all x1 -> x0, starting transfers between devices: 5.63 us -> none  [shards(): lax.all_to_all(outgoing, 'bal', split_axis=0, concat_axis=0, tiled=True)]
    ppermute x0 -> x3, starting transfers between devices: none -> 4.99 us  [swapped_with_each(): done.append(lax.ppermute(sent, axis, [(i, i ^ step) for i in range(peers)]))]
    gather x0 -> x1, local copies, waits for them, and re-layouts: none -> 1.65 us  [swapped_with_each(): blocks = jnp.stack(done)[index ^ jnp.arange(peers)]]
  transfers between devices with their start and end apart: 5 -> 7, of which waited for: 5 -> 6; matrix products, arithmetic and copies ran while one was open for 3% -> 4% of each run, Pallas kernels for 0% -> 0%
where the time goes in v1:
time: 130 us; the launch traced here: 127 us
  waiting for transfers between devices  48.6 us (37%)
  other arithmetic  44.6 us (34%)
  local copies, waits for them, and re-layouts  17.1 us (13%)
  starting transfers between devices  11.3 us (9%)
  matrix products  4.52 us (3%)
    scatter-add x8, other arithmetic, shards(): sent = sent.at[ext_index[:, column]].add(flux)  20.9 us
    ppermute x3, waiting for transfers between devices, swapped_with_each(): done.append(lax.ppermute(sent, axis, [(i, i ^ step) for i in range(peers)]))  17.9 us
    ppermute x1, waiting for transfers between devices, extended_2(): lax.ppermute(tail, axis, [(i, (i + 1) % count) for i in range(count)])  17.5 us
    gather x8, local copies, waits for them, and re-layouts, shards(): extended[ext_index[:, column]] - own_blocks  12.9 us
    ppermute x2, waiting for transfers between devices, shifted(): return lax.ppermute(value, axis, pairs)  12.6 us
    mul x1, other arithmetic, shards(): coefs[:, column][:, None, None]  7.75 us
    scatter x1, other arithmetic, shards(): jnp.zeros((bal_count * capacity, width), jnp.bfloat16).at[slot]  6.05 us
    ppermute x3, starting transfers between devices, swapped_with_each(): done.append(lax.ppermute(sent, axis, [(i, i ^ step) for i in range(peers)]))  4.99 us
  transfers between devices with their start and end apart: 7, of which 6 were waited for; matrix products, arithmetic and copies ran while one was open for 4% of the time, Pallas kernels for 0%

profile of v1, /device:TPU:0, one launch (start us, length us, event | category | flops | bytes accessed | tf_op | source)
XLA Modules:
  0.0 127.5 jit_solution(8874972701164417663)
XLA Ops:
  0.6 0.5 collective-permute-start
  1.2 2.9 %collective-permute-start.1 = (f32[16,128,128]{2,1,0:T(8,128)}, f32[16,128,128]{2,1,0:T(8,128)}, u32[]{:S(2)}, u32[]{:S(2)}) collective-permute-start(f32[16,128,128]{2,1,0:T(8,128)} %bitcast.82), channel_id=1, source_target_pairs={{4,0},{8,4},{12,8},{16,12},{20,16},{24,20},{28,24},{0,28},{5,1},{9... | collective-permute-start | bytes 3145736 | tf_op jit(solution)/shard_map/ppermute | solution.py:43
  4.1 0.7 fusion.19
  4.9 0.7 fusion.15
  5.6 1.1 reduce-window.6
  6.7 0.2 slice_reduce_fusion
  6.9 0.2 reduce-window.9
  7.2 0.7 multiply_select_fusion
  7.9 0.1 add_bitcast_fusion
  7.9 17.5 %collective-permute-done = f32[16,128,128]{2,1,0:T(8,128)S(1)} collective-permute-done((f32[16,128,128]{2,1,0:T(8,128)}, f32[16,128,128]{2,1,0:T(8,128)S(1)}, u32[]{:S(2)}, u32[]{:S(2)}) %collective-permute-start) | collective-permute-done | bytes 1048608 | tf_op jit(solution)/shard_map/ppermute | solution.py:41
  25.4 1.0 copy-done.7
  26.4 0.6 collective-permute-done.1
  27.0 2.1 %pad_maximum_fusion = f32[48,128,128]{2,1,0:T(8,128)S(1)} fusion(f32[16,128,128]{2,1,0:T(8,128)} %collective-permute-done.1, f32[16,128,128]{2,1,0:T(8,128)} %bitcast.83, f32[16,128,128]{2,1,0:T(8,128)} %copy-done.7), kind=kLoop, calls=%fused_computation.22 | loop fusion | flops 1572864 | bytes 6291456 | tf_op jit(solution)/shard_map/concatenate | solution.py:39
  29.0 1.6 %gather_fusion = f32[16,128,128]{2,1,0:T(8,128)} fusion(f32[48,128,128]{2,1,0:T(8,128)S(1)} %pad_maximum_fusion, s32[1024]{0:T(1024)S(1)} %get-tuple-element.63), kind=kCustom, calls=%fused_computation | custom fusion | bytes 2097216 | tf_op jit(solution)/shard_map/gather | solution.py:86
  30.6 1.6 %gather_fusion.1 = f32[16,128,128]{2,1,0:T(8,128)} fusion(f32[48,128,128]{2,1,0:T(8,128)S(1)} %pad_maximum_fusion, s32[1024]{0:T(1024)S(1)} %get-tuple-element.62), kind=kCustom, calls=%fused_computation.1 | custom fusion | bytes 2097216 | tf_op jit(solution)/shard_map/gather | solution.py:86
  32.3 1.6 %gather_fusion.2 = f32[16,128,128]{2,1,0:T(8,128)} fusion(f32[48,128,128]{2,1,0:T(8,128)S(1)} %pad_maximum_fusion, s32[1024]{0:T(1024)S(1)} %get-tuple-element.61), kind=kCustom, calls=%fused_computation.2 | custom fusion | bytes 2097216 | tf_op jit(solution)/shard_map/gather | solution.py:86
  33.9 1.6 %gather_fusion.3 = f32[16,128,128]{2,1,0:T(8,128)} fusion(f32[48,128,128]{2,1,0:T(8,128)S(1)} %pad_maximum_fusion, s32[1024]{0:T(1024)S(1)} %get-tuple-element.60), kind=kCustom, calls=%fused_computation.3 | custom fusion | bytes 2097216 | tf_op jit(solution)/shard_map/gather | solution.py:86
  35.5 1.6 %gather_fusion.4 = f32[16,128,128]{2,1,0:T(8,128)} fusion(f32[48,128,128]{2,1,0:T(8,128)S(1)} %pad_maximum_fusion, s32[1024]{0:T(1024)S(1)} %get-tuple-element.59), kind=kCustom, calls=%fused_computation.4 | custom fusion | bytes 2097216 | tf_op jit(solution)/shard_map/gather | solution.py:86
  37.1 1.6 %gather_fusion.5 = f32[16,128,128]{2,1,0:T(8,128)} fusion(f32[48,128,128]{2,1,0:T(8,128)S(1)} %pad_maximum_fusion, s32[1024]{0:T(1024)S(1)} %get-tuple-element.58), kind=kCustom, calls=%fused_computation.5 | custom fusion | bytes 2097216 | tf_op jit(solution)/shard_map/gather | solution.py:86
  38.7 1.6 %gather_fusion.6 = f32[16,128,128]{2,1,0:T(8,128)} fusion(f32[48,128,128]{2,1,0:T(8,128)S(1)} %pad_maximum_fusion, s32[1024]{0:T(1024)S(1)} %get-tuple-element.57), kind=kCustom, calls=%fused_computation.6 | custom fusion | bytes 2097216 | tf_op jit(solution)/shard_map/gather | solution.py:86
  40.3 1.6 %gather_fusion.7 = f32[16,128,128]{2,1,0:T(8,128)} fusion(f32[48,128,128]{2,1,0:T(8,128)S(1)} %pad_maximum_fusion, s32[1024]{0:T(1024)S(1)} %get-tuple-element.56), kind=kCustom, calls=%fused_computation.7 | custom fusion | bytes 2097216 | tf_op jit(solution)/shard_map/gather | solution.py:86
  41.9 7.7 %subtract_multiply_fusion = (f32[16,128,128]{2,1,0:T(8,128)}, f32[16,128,128]{2,1,0:T(8,128)}, f32[16,128,128]{2,1,0:T(8,128)}, f32[16,128,128]{2,1,0:T(8,128)},...) fusion(f32[16,128,128]{2,1,0:T(8,128)} %gather_fusion.7, ...), kind=kLoop, calls=%fused_computation.33 | loop fusion | flops 4194304 | bytes 17826304 | tf_op jit(solution)/shard_map/mul | solution.py:86
  49.6 0.4 broadcast_in_dim.15
  50.0 2.6 %scatter_fusion = f32[48,128,128]{2,1,0:T(8,128)S(1)} fusion(f32[48,128,128]{2,1,0:T(8,128)S(1)} %broadcast_in_dim.15, s32[16]{0:T(128)S(1)} %get-tuple-element.55, f32[16,128,128]{2,1,0:T(8,128)} %get-tuple-element.39), kind=kCustom, calls=%fused_computation.9 | custom fusion | flops 262144 | bytes 3145792 | tf_op jit(solution)/shard_map/scatter-add | solution.py:88
  52.6 2.6 %scatter_fusion.1 = f32[48,128,128]{2,1,0:T(8,128)S(1)} fusion(f32[48,128,128]{2,1,0:T(8,128)S(1)} %scatter_fusion, s32[16]{0:T(128)S(1)} %get-tuple-element.54, f32[16,128,128]{2,1,0:T(8,128)} %get-tuple-element.38), kind=kCustom, calls=%fused_computation.10 | custom fusion | flops 262144 | bytes 3145792 | tf_op jit(solution)/shard_map/scatter-add | solution.py:88
  55.2 2.6 %scatter_fusion.2 = f32[48,128,128]{2,1,0:T(8,128)S(1)} fusion(f32[48,128,128]{2,1,0:T(8,128)S(1)} %scatter_fusion.1, s32[16]{0:T(128)S(1)} %get-tuple-element.53, f32[16,128,128]{2,1,0:T(8,128)} %get-tuple-element.37), kind=kCustom, calls=%fused_computation.11 | custom fusion | flops 262144 | bytes 3145792 | tf_op jit(solution)/shard_map/scatter-add | solution.py:88
  57.8 2.6 %scatter_fusion.3 = f32[48,128,128]{2,1,0:T(8,128)S(1)} fusion(f32[48,128,128]{2,1,0:T(8,128)S(1)} %scatter_fusion.2, s32[16]{0:T(128)S(1)} %get-tuple-element.52, f32[16,128,128]{2,1,0:T(8,128)} %get-tuple-element.36), kind=kCustom, calls=%fused_computation.12 | custom fusion | flops 262144 | bytes 3145792 | tf_op jit(solution)/shard_map/scatter-add | solution.py:88
  60.5 2.6 %scatter_fusion.4 = f32[48,128,128]{2,1,0:T(8,128)S(1)} fusion(f32[48,128,128]{2,1,0:T(8,128)S(1)} %scatter_fusion.3, s32[16]{0:T(128)S(1)} %get-tuple-element.51, f32[16,128,128]{2,1,0:T(8,128)} %get-tuple-element.35), kind=kCustom, calls=%fused_computation.13 | custom fusion | flops 262144 | bytes 3145792 | tf_op jit(solution)/shard_map/scatter-add | solution.py:88
  63.1 2.6 %scatter_fusion.5 = f32[48,128,128]{2,1,0:T(8,128)S(1)} fusion(f32[48,128,128]{2,1,0:T(8,128)S(1)} %scatter_fusion.4, s32[16]{0:T(128)S(1)} %get-tuple-element.50, f32[16,128,128]{2,1,0:T(8,128)} %get-tuple-element.34), kind=kCustom, calls=%fused_computation.14 | custom fusion | flops 262144 | bytes 3145792 | tf_op jit(solution)/shard_map/scatter-add | solution.py:88
  65.7 2.6 %scatter_fusion.6 = f32[48,128,128]{2,1,0:T(8,128)S(1)} fusion(f32[48,128,128]{2,1,0:T(8,128)S(1)} %scatter_fusion.5, s32[16]{0:T(128)S(1)} %get-tuple-element.49, f32[16,128,128]{2,1,0:T(8,128)} %get-tuple-element.33), kind=kCustom, calls=%fused_computation.15 | custom fusion | flops 262144 | bytes 3145792 | tf_op jit(solution)/shard_map/scatter-add | solution.py:88
  68.3 2.6 %scatter_fusion.7 = f32[48,128,128]{2,1,0:T(8,128)S(1)} fusion(f32[48,128,128]{2,1,0:T(8,128)S(1)} %scatter_fusion.6, s32[16]{0:T(128)S(1)} %get-tuple-element.48, f32[16,128,128]{2,1,0:T(8,128)} %get-tuple-element.32), kind=kCustom, calls=%fused_computation.16 | custom fusion | flops 262144 | bytes 3145792 | tf_op jit(solution)/shard_map/scatter-add | solution.py:88
  71.0 0.3 convert.4
  71.3 0.1 fusion.30
  71.3 2.9 %collective-permute-start.2 = (bf16[16,128,128]{2,1,0:T(8,128)(2,1)S(1)}, bf16[16,128,128]{2,1,0:T(8,128)(2,1)S(1)}, u32[]{:S(2)}, u32[]{:S(2)}) collective-permute-start(bf16[16,128,128]{2,1,0:T(8,128)(2,1)S(1)} %get-tuple-element.26), channel_id=1, source_target_pairs={{0,28},{4,0},{8,4},{12,8},{16,12},{20,16},{24,20},{28,24},{1,29},{... | collective-permute-start | bytes 1572872 | tf_op jit(solution)/shard_map/ppermute | solution.py:53
  74.3 12.2 %collective-permute-done.2 = bf16[16,128,128]{2,1,0:T(8,128)(2,1)S(1)} collective-permute-done((bf16[16,128,128]{2,1,0:T(8,128)(2,1)S(1)}, bf16[16,128,128]{2,1,0:T(8,128)(2,1)S(1)}, u32[]{:S(2)}, u32[]{:S(2)}) %collective-permute-start.2) | collective-permute-done | bytes 524320 | tf_op jit(solution)/shard_map/ppermute | solution.py:53
  86.5 0.4 collective-permute-done.3
  87.0 3.1 %fusion.6 = f32[16,128,128]{2,1,0:T(8,128)S(1)} fusion(f32[16,128,128]{2,1,0:T(8,128)} %bitcast.85, f32[48,128,128]{2,1,0:T(8,128)S(1)} %scatter_fusion.7, bf16[16,128,128]{2,1,0:T(8,128)(2,1)S(1)} %collective-permute-done.3, bf16[16,128,128]{2,1,0:T(8,128)(2,1)S(1)} %collective-permute-done.2, f32[16,128,128]{2,1,0:T(8,128)S(1)} %copy-done.1, ...), kind=kLoop, calls=%fused_computation.28 | loop fusion | flops 3407872 | bytes 12582912 | tf_op jit(solution)/shard_map/add | solution.py:92
  90.1 1.1 fusion.8
  91.1 4.7 %while.10 = (s32[]{:T(128)}, f32[2048,128]{1,0:T(8,128)S(1)}, bf16[128,128]{1,0:T(8,128)(2,1)S(1)}, s32[]{:T(128)}) while((s32[]{:T(128)}, f32[2048,128]{1,0:T(8,128)S(1)}, bf16[128,128]{1,0:T(8,128)(2,1)S(1)}, s32[]{:T(128)}) %tuple.54), condition=%wide.region_9.10_spmd, body=%wide.region_8.9_spmd.sunk | while | flops 67895296 | bytes 4227125 | solution.py:64
  91.2 0.1 copy.28
  91.2 0.3 fusion.39
  91.6 0.3 fusion.39
  92.0 0.3 fusion.39
  92.3 0.1 copy.28
  92.4 0.3 fusion.39
  92.7 0.1 copy.28
  92.8 0.3 fusion.39
  93.2 0.3 fusion.39
  93.5 0.1 copy.28
  93.6 0.3 fusion.39
  93.9 0.3 fusion.39
  94.3 0.3 fusion.39
  94.7 0.3 fusion.39
  95.1 0.3 fusion.39
  95.5 0.3 fusion.39
  95.8 6.0 %scatter_custom_fusion.8 = bf16[4096,128]{1,0:T(8,128)(2,1)S(1)} fusion(s32[2048]{0:T(1024)S(1)} %bitcast.94, bf16[]{:T(256)} %constant.81.clone.1, f32[2048,128]{1,0:T(8,128)S(1)} %get-tuple-element.19), kind=kCustom, calls=%fused_computation.42 | custom fusion | flops 262144 | bytes 2097154 | tf_op jit(solution)/shard_map/scatter | solution.py:104
  101.9 0.1 constant_dynamic-slice_fusion
  102.0 2.4 %collective-permute-start.4 = (bf16[1,1024,128]{2,1,0:T(8,128)(2,1)S(1)}, bf16[1,1024,128]{2,1,0:T(8,128)(2,1)S(1)}, u32[]{:S(2)}, u32[]{:S(2)}) collective-permute-start(bf16[1,1024,128]{2,1,0:T(8,128)(2,1)S(1)} %get-tuple-element.31), channel_id=1, source_target_pairs={{0,1},{1,0},{2,3},{3,2},{4,5},{5,4},{6,7},{7,6},{8,9},{9,8},{10,11... | collective-permute-start | bytes 786440 | tf_op jit(solution)/shard_map/ppermute | solution.py:29
  104.4 2.6 %collective-permute-start.5 = (bf16[1,1024,128]{2,1,0:T(8,128)(2,1)S(1)}, bf16[1,1024,128]{2,1,0:T(8,128)(2,1)S(1)}, u32[]{:S(2)}, u32[]{:S(2)}) collective-permute-start(bf16[1,1024,128]{2,1,0:T(8,128)(2,1)S(1)} %get-tuple-element.30), channel_id=1, source_target_pairs={{0,2},{1,3},{2,0},{3,1},{4,6},{5,7},{6,4},{7,5},{8,10},{9,11},{10,... | collective-permute-start | bytes 786440 | tf_op jit(solution)/shard_map/ppermute | solution.py:29
  107.0 0.8 convert_element_type.36
  107.8 6.6 %collective-permute-done.4 = bf16[1,1024,128]{2,1,0:T(8,128)(2,1)S(1)} collective-permute-done((bf16[1,1024,128]{2,1,0:T(8,128)(2,1)S(1)}, bf16[1,1024,128]{2,1,0:T(8,128)(2,1)S(1)}, u32[]{:S(2)}, u32[]{:S(2)}) %collective-permute-start.4) | collective-permute-done | bytes 262176 | tf_op jit(solution)/shard_map/ppermute | solution.py:29
  114.4 11.3 %collective-permute-done.5 = bf16[1,1024,128]{2,1,0:T(8,128)(2,1)S(1)} collective-permute-done((bf16[1,1024,128]{2,1,0:T(8,128)(2,1)S(1)}, bf16[1,1024,128]{2,1,0:T(8,128)(2,1)S(1)}, u32[]{:S(2)}, u32[]{:S(2)}) %collective-permute-start.5) | collective-permute-done | bytes 262176 | tf_op jit(solution)/shard_map/ppermute | solution.py:29
  125.7 0.1 maximum_bitcast_fusion
  125.8 1.7 %gather_fusion.8 = bf16[4,1024,128]{2,1,0:T(8,128)(2,1)} fusion(bf16[4,1024,128]{2,1,0:T(8,128)(2,1)S(1)} %maximum_bitcast_fusion, s32[1024]{0:T(1024)S(1)} %pad_clamp_fusion), kind=kCustom, calls=%fused_computation.8 | custom fusion | bytes 2097168 | tf_op jit(solution)/shard_map/gather | solution.py:30
  (42 shorter events, 0.7 us)
Async XLA Ops:
  0.6 89.4 %copy-start = (f32[32,128]{1,0:T(8,128)S(1)}, f32[32,128]{1,0:T(8,128)}, u32[]{:S(2)}) copy-start(f32[32,128]{1,0:T(8,128)} %param.16) | copy-start | bytes 49156
  0.6 24.8 %collective-permute-start = (f32[16,128,128]{2,1,0:T(8,128)}, f32[16,128,128]{2,1,0:T(8,128)S(1)}, u32[]{:S(2)}, u32[]{:S(2)}) collective-permute-start(f32[16,128,128]{2,1,0:T(8,128)} %bitcast.81), channel_id=1, source_target_pairs={{0,4},{4,8},{8,12},{12,16},{16,20},{20,24},{24,28},{28,0},{1,5},{5... | collective-permute-start | bytes 3145736 | tf_op jit(solution)/shard_map/ppermute | solution.py:41
  1.2 25.8 %collective-permute-start.1 = (f32[16,128,128]{2,1,0:T(8,128)}, f32[16,128,128]{2,1,0:T(8,128)}, u32[]{:S(2)}, u32[]{:S(2)}) collective-permute-start(f32[16,128,128]{2,1,0:T(8,128)} %bitcast.82), channel_id=1, source_target_pairs={{4,0},{8,4},{12,8},{16,12},{20,16},{24,20},{28,24},{0,28},{5,1},{9... | collective-permute-start | bytes 3145736 | tf_op jit(solution)/shard_map/ppermute | solution.py:43
  25.4 1.0 copy-start.7
  70.9 3.3 %copy-start.9 = (s32[2048,1]{0,1:T(1,128)S(1)}, s32[2048,1]{0,1:T(1,128)}, u32[]{:S(2)}) copy-start(s32[2048,1]{0,1:T(1,128)} %param.15) | copy-start | bytes 24580
  70.9 16.0 %copy-start.1 = (f32[16,128,128]{2,1,0:T(8,128)S(1)}, f32[16,128,128]{2,1,0:T(8,128)}, u32[]{:S(2)}) copy-start(f32[16,128,128]{2,1,0:T(8,128)} %get-tuple-element.32) | copy-start | bytes 3145732
  70.9 16.0 %copy-start.2 = (f32[16,128,128]{2,1,0:T(8,128)S(1)}, f32[16,128,128]{2,1,0:T(8,128)}, u32[]{:S(2)}) copy-start(f32[16,128,128]{2,1,0:T(8,128)} %get-tuple-element.33) | copy-start | bytes 3145732
  71.0 16.0 %copy-start.3 = (f32[16,128,128]{2,1,0:T(8,128)S(1)}, f32[16,128,128]{2,1,0:T(8,128)}, u32[]{:S(2)}) copy-start(f32[16,128,128]{2,1,0:T(8,128)} %get-tuple-element.34) | copy-start | bytes 3145732
  71.0 16.0 %copy-start.4 = (f32[16,128,128]{2,1,0:T(8,128)S(1)}, f32[16,128,128]{2,1,0:T(8,128)}, u32[]{:S(2)}) copy-start(f32[16,128,128]{2,1,0:T(8,128)} %get-tuple-element.35) | copy-start | bytes 3145732
  71.0 16.0 %copy-start.5 = (f32[16,128,128]{2,1,0:T(8,128)S(1)}, f32[16,128,128]{2,1,0:T(8,128)}, u32[]{:S(2)}) copy-start(f32[16,128,128]{2,1,0:T(8,128)} %get-tuple-element.36) | copy-start | bytes 3145732
  71.0 16.0 %copy-start.6 = (f32[16,128,128]{2,1,0:T(8,128)S(1)}, f32[16,128,128]{2,1,0:T(8,128)}, u32[]{:S(2)}) copy-start(f32[16,128,128]{2,1,0:T(8,128)} %get-tuple-element.37) | copy-start | bytes 3145732
  71.3 15.2 %collective-permute-start.2 = (bf16[16,128,128]{2,1,0:T(8,128)(2,1)S(1)}, bf16[16,128,128]{2,1,0:T(8,128)(2,1)S(1)}, u32[]{:S(2)}, u32[]{:S(2)}) collective-permute-start(bf16[16,128,128]{2,1,0:T(8,128)(2,1)S(1)} %get-tuple-element.26), channel_id=1, source_target_pairs={{0,28},{4,0},{8,4},{12,8},{16,12},{20,16},{24,20},{28,24},{1,29},{... | collective-permute-start | bytes 1572872 | tf_op jit(solution)/shard_map/ppermute | solution.py:53
  74.2 12.7 %collective-permute-start.3 = (bf16[16,128,128]{2,1,0:T(8,128)(2,1)S(1)}, bf16[16,128,128]{2,1,0:T(8,128)(2,1)S(1)}, u32[]{:S(2)}, u32[]{:S(2)}) collective-permute-start(bf16[16,128,128]{2,1,0:T(8,128)(2,1)S(1)} %get-tuple-element.27), channel_id=1, source_target_pairs={{0,4},{4,8},{8,12},{12,16},{16,20},{20,24},{24,28},{28,0},{1,5},{5... | collective-permute-start | bytes 1572872 | tf_op jit(solution)/shard_map/ppermute | solution.py:53
  74.3 15.8 %copy-start.10 = (s32[2048]{0:T(1024)S(1)}, s32[2048]{0:T(1024)}, u32[]{:S(2)}) copy-start(s32[2048]{0:T(1024)} %param.14) | copy-start | bytes 24580
  74.3 16.8 %copy-start.8 = (bf16[128,128]{1,0:T(8,128)(2,1)S(1)}, bf16[128,128]{1,0:T(8,128)(2,1)}, u32[]{:S(2)}) copy-start(bf16[128,128]{1,0:T(8,128)(2,1)} %param.17) | copy-start | bytes 98308
  102.0 12.4 %collective-permute-start.4 = (bf16[1,1024,128]{2,1,0:T(8,128)(2,1)S(1)}, bf16[1,1024,128]{2,1,0:T(8,128)(2,1)S(1)}, u32[]{:S(2)}, u32[]{:S(2)}) collective-permute-start(bf16[1,1024,128]{2,1,0:T(8,128)(2,1)S(1)} %get-tuple-element.31), channel_id=1, source_target_pairs={{0,1},{1,0},{2,3},{3,2},{4,5},{5,4},{6,7},{7,6},{8,9},{9,8},{10,11... | collective-permute-start | bytes 786440 | tf_op jit(solution)/shard_map/ppermute | solution.py:29
  104.4 21.3 %collective-permute-start.5 = (bf16[1,1024,128]{2,1,0:T(8,128)(2,1)S(1)}, bf16[1,1024,128]{2,1,0:T(8,128)(2,1)S(1)}, u32[]{:S(2)}, u32[]{:S(2)}) collective-permute-start(bf16[1,1024,128]{2,1,0:T(8,128)(2,1)S(1)} %get-tuple-element.30), channel_id=1, source_target_pairs={{0,2},{1,3},{2,0},{3,1},{4,6},{5,7},{6,4},{7,5},{8,10},{9,11},{10,... | collective-permute-start | bytes 786440 | tf_op jit(solution)/shard_map/ppermute | solution.py:29
  106.9 18.7 %collective-permute-start.6 = (bf16[1,1024,128]{2,1,0:T(8,128)(2,1)S(1)}, bf16[1,1024,128]{2,1,0:T(8,128)(2,1)S(1)}, u32[]{:S(2)}, u32[]{:S(2)}) collective-permute-start(bf16[1,1024,128]{2,1,0:T(8,128)(2,1)S(1)} %get-tuple-element.29), channel_id=1, source_target_pairs={{0,3},{1,2},{2,1},{3,0},{4,7},{5,6},{6,5},{7,4},{8,11},{9,10},{10,... | collective-permute-start | bytes 786440 | tf_op jit(solution)/shard_map/ppermute | solution.py:29
